TPU v7x, 128 devices: a whole 4x4x4 slice. The times are simulated.
128 devices in a mesh: ctx: 8 (over x, z_lo), fsdp: 16 (over z_hi, y, core).
Axes of the slice: x: 4, y: 4, z: 4 (z_hi: 2, z_lo: 2; z = z_hi * 2 + z_lo), core: 2. Of those that a mesh axis runs over, the one named last changes fastest.
Arguments:
- inputs: bfloat16 [16, 1024, 1152], P('fsdp', 'ctx'), may hold values from -6 to 6
- out_grad: bfloat16 [16, 1024, 1152], P('fsdp', 'ctx'), may hold values from -6 to 6
- positions: int32 [16, 1024], P('fsdp', 'ctx'), may hold values from 0 to 1023, as said below
- block_order: int32 [8, 2], replicated, may hold values from 0 to 15, as said below
- w_query: bfloat16 [1152, 1024], P('fsdp'), may hold values from -0.1875 to 0.1875
- w_key: bfloat16 [1152, 256], P('fsdp'), may hold values from -0.1875 to 0.1875
- w_value: bfloat16 [1152, 256], P('fsdp'), may hold values from -0.1875 to 0.1875
- w_output: bfloat16 [1024, 1152], P(None, 'fsdp'), may hold values from -0.1875 to 0.1875
- w_gate: bfloat16 [6912, 1152], P('fsdp'), may hold values from -0.1875 to 0.1875
- w_up: bfloat16 [6912, 1152], P('fsdp'), may hold values from -0.1875 to 0.1875
- w_down: bfloat16 [6912, 1152], P('fsdp'), may hold values from -0.078125 to 0.078125
- gain_in: bfloat16 [1152], P('fsdp'), may hold values from 0.099609375 to 1.8984375
- gain_query: bfloat16 [256], P('fsdp'), may hold values from 0.099609375 to 1.8984375
- gain_key: bfloat16 [256], P('fsdp'), may hold values from 0.099609375 to 1.8984375
- gain_attn: bfloat16 [1152], P('fsdp'), may hold values from 0.099609375 to 1.8984375
- gain_pre: bfloat16 [1152], P('fsdp'), may hold values from 0.099609375 to 1.8984375
- gain_post: bfloat16 [1152], P('fsdp'), may hold values from 0.099609375 to 1.8984375
Outputs:
- outputs: bfloat16 [16, 1024, 1152], P('fsdp', 'ctx')
- in_grad: bfloat16 [16, 1024, 1152], P('fsdp', 'ctx')
- grad_w_query: float32 [1152, 1024], P('fsdp')
- grad_w_key: float32 [1152, 256], P('fsdp')
- grad_w_value: float32 [1152, 256], P('fsdp')
- grad_w_output: float32 [1024, 1152], P(None, 'fsdp')
- grad_w_gate: float32 [6912, 1152], P('fsdp')
- grad_w_up: float32 [6912, 1152], P('fsdp')
- grad_w_down: float32 [6912, 1152], P('fsdp')
- grad_gain_in: float32 [1152], P('fsdp')
- grad_gain_query: float32 [256], P('fsdp')
- grad_gain_key: float32 [256], P('fsdp')
- grad_gain_attn: float32 [1152], P('fsdp')
- grad_gain_pre: float32 [1152], P('fsdp')
- grad_gain_post: float32 [1152], P('fsdp')
Inputs may be any that keep to these rules, and one draw needn't show every extreme that they name: `block_order`: row c names the two blocks of 64 tokens in device c's rows, in order; every block appears once, and a row holds blocks k and m with k + m one less than the number of blocks. `positions`: each row's offset from the start of its document in the sequence; documents begin at the sequence's first token and at random places; sequence 0 is one document.
All inputs are finite; a program needn't handle non-finite values.
Results may differ from a plain program's by a relative error of at most 0.03.
Values may be sent and summed in bfloat16 or wider, within the bound.
No kernel may reach another device: no remote copies, remote signals or barrier semaphores. Data moves between devices by JAX's collectives and lax.ppermute only.
A program may use at most 128 MiB of HBM per device.

v0:
```python
import jax
import jax.numpy as jnp
from jax import lax
from jax.sharding import PartitionSpec as P

H = 4
HD = 256
EPS = 1e-06
ROPE_BASE = 1000000.0
GELU_C = 0.7978845608028654
GELU_A = 0.044715


def norm_forward(values, gain):
    inverse = lax.rsqrt(jnp.mean(values * values, axis=-1, keepdims=True) + EPS)
    unit = values * inverse
    return (unit * gain, unit, inverse)


def norm_backward(upstream, unit, inverse, gain):
    scaled = upstream * gain
    inner = jnp.mean(scaled * unit, axis=-1, keepdims=True)
    leading = tuple(range(upstream.ndim - 1))
    return (inverse * (scaled - unit * inner), jnp.sum(upstream * unit, axis=leading))


def gelu_pair(gate):
    inner = GELU_C * (gate + GELU_A * gate * gate * gate)
    tangent = jnp.tanh(inner)
    value = 0.5 * gate * (1.0 + tangent)
    slope = 0.5 * (1.0 + tangent) + 0.5 * gate * (1.0 - tangent * tangent) * GELU_C * (
        1.0 + 3.0 * GELU_A * gate * gate
    )
    return (value, slope)


def rope_tables(positions, width):
    half = width // 2
    freqs = ROPE_BASE ** (-2.0 * jnp.arange(half, dtype=jnp.float32) / width)
    angles = positions.astype(jnp.float32)[:, None] * freqs[None, :]
    return (jnp.cos(angles), jnp.sin(angles))


def rotate(values, cosine, sine):
    half = values.shape[-1] // 2
    first = values[..., :half]
    second = values[..., half:]
    return jnp.concatenate(
        [first * cosine - second * sine, second * cosine + first * sine], axis=-1
    )


def rotate_back(values, cosine, sine):
    half = values.shape[-1] // 2
    first = values[..., :half]
    second = values[..., half:]
    return jnp.concatenate(
        [first * cosine + second * sine, second * cosine - first * sine], axis=-1
    )


def sequence_rows(order_flat, first_row, count, block):
    rows = first_row + jnp.arange(count, dtype=jnp.int32)
    slots = rows // block
    table = jnp.arange(order_flat.shape[0], dtype=jnp.int32)
    picked = jnp.sum(jnp.where(slots[:, None] == table[None, :], order_flat[None, :], 0), axis=1)
    return picked * block + rows % block


def body(
    inputs,
    out_grad,
    positions,
    block_order,
    w_query,
    w_key,
    w_value,
    w_output,
    w_gate,
    w_up,
    w_down,
    gain_in,
    gain_query,
    gain_key,
    gain_attn,
    gain_pre,
    gain_post,
):
    f32 = jnp.float32
    low = jnp.bfloat16
    tokens = inputs[0]
    local = tokens.shape[0]
    parts = lax.axis_size("ctx")
    total = local * parts
    block = local // 2
    gathered = (
        lax.all_gather(w_query, "fsdp", axis=0, tiled=True),
        lax.all_gather(w_key, "fsdp", axis=0, tiled=True),
        lax.all_gather(w_value, "fsdp", axis=0, tiled=True),
        lax.all_gather(w_output, "fsdp", axis=1, tiled=True),
        lax.all_gather(gain_in, "fsdp", axis=0, tiled=True),
        lax.all_gather(gain_query, "fsdp", axis=0, tiled=True),
        lax.all_gather(gain_key, "fsdp", axis=0, tiled=True),
        lax.all_gather(gain_attn, "fsdp", axis=0, tiled=True),
        lax.all_gather(gain_pre, "fsdp", axis=0, tiled=True),
        lax.all_gather(gain_post, "fsdp", axis=0, tiled=True),
    )
    full_query, full_key, full_value, full_output = (
        gathered[0],
        gathered[1],
        gathered[2],
        gathered[3],
    )
    norm_in, norm_query, norm_key, norm_attn, norm_pre, norm_post = [
        g.astype(f32) for g in gathered[4:]
    ]
    ctx_index = lax.axis_index("ctx")
    order_flat = block_order.reshape(-1)
    my_seq = sequence_rows(order_flat, ctx_index * local, local, block)
    all_seq = sequence_rows(order_flat, 0, total, block)
    flat_in = tokens.astype(f32)
    normed_full, unit_in, inv_in = norm_forward(flat_in, norm_in)
    normed_in = normed_full.astype(low)
    queries = jnp.dot(normed_in, full_query, preferred_element_type=f32).reshape(local, H, HD)
    keys_raw = jnp.dot(normed_in, full_key, preferred_element_type=f32)
    values = jnp.dot(normed_in, full_value, preferred_element_type=f32).astype(low)
    query_normed, query_unit, query_inv = norm_forward(queries, norm_query)
    key_normed, key_unit, key_inv = norm_forward(keys_raw, norm_key)
    cosine, sine = rope_tables(positions[0], HD)
    scale = HD ** (-0.5)
    query_rot = (rotate(query_normed, cosine[:, None, :], sine[:, None, :]) * scale).astype(low)
    key_rot = rotate(key_normed, cosine, sine).astype(low)
    key_all, value_all = (
        lax.all_gather(key_rot, "ctx", axis=0, tiled=True),
        lax.all_gather(values, "ctx", axis=0, tiled=True),
    )
    scores = jnp.einsum("qhd,kd->hqk", query_rot, key_all, preferred_element_type=f32)
    allowed = my_seq[:, None] >= all_seq[None, :]
    scores = jnp.where(allowed[None], scores, -jnp.inf)
    highest = jnp.max(scores, axis=-1, keepdims=True)
    log_total = highest + jnp.log(jnp.sum(jnp.exp(scores - highest), axis=-1, keepdims=True))
    probs_full = jnp.exp(scores - log_total)
    probs = probs_full.astype(low)
    attended = (
        jnp.einsum("hqk,kd->qhd", probs, value_all, preferred_element_type=f32)
        .reshape(local, H * HD)
        .astype(low)
    )
    branch_attn = jnp.dot(attended, full_output, preferred_element_type=f32)
    attn_normed, attn_unit, attn_inv = norm_forward(branch_attn, norm_attn)
    residual = flat_in + attn_normed
    pre_full, pre_unit, pre_inv = norm_forward(residual, norm_pre)
    normed_pre = pre_full.astype(low)
    rows_all = lax.all_gather(normed_pre, "fsdp", axis=0, tiled=True)
    gate = jnp.einsum("td,fd->tf", rows_all, w_gate, preferred_element_type=f32)
    upper = jnp.einsum("td,fd->tf", rows_all, w_up, preferred_element_type=f32)
    gelu_value, gelu_slope = gelu_pair(gate)
    hidden = (gelu_value * upper).astype(low)
    branch_ffn = lax.psum_scatter(
        jnp.dot(hidden, w_down, preferred_element_type=f32).astype(jnp.bfloat16),
        "fsdp",
        scatter_dimension=0,
        tiled=True,
    ).astype(jnp.float32)
    post_normed, post_unit, post_inv = norm_forward(branch_ffn, norm_post)
    outputs = (residual + post_normed).astype(low)
    grad_out = out_grad[0].astype(f32)
    grad_ffn_full, grad_gain_post = norm_backward(grad_out, post_unit, post_inv, norm_post)
    grad_ffn = grad_ffn_full.astype(low)
    grad_all = lax.all_gather(grad_ffn, "fsdp", axis=0, tiled=True)
    grad_hidden = jnp.einsum("td,fd->tf", grad_all, w_down, preferred_element_type=f32)
    grad_gate = (grad_hidden * upper * gelu_slope).astype(low)
    grad_up = (grad_hidden * gelu_value).astype(low)
    shard_gate = jnp.einsum("tf,td->fd", grad_gate, rows_all, preferred_element_type=f32)
    shard_up = jnp.einsum("tf,td->fd", grad_up, rows_all, preferred_element_type=f32)
    shard_down = jnp.einsum("tf,td->fd", hidden, grad_all, preferred_element_type=f32)
    grad_pre = lax.psum_scatter(
        (
            jnp.dot(grad_gate, w_gate, preferred_element_type=f32)
            + jnp.dot(grad_up, w_up, preferred_element_type=f32)
        ).astype(jnp.bfloat16),
        "fsdp",
        scatter_dimension=0,
        tiled=True,
    ).astype(jnp.float32)
    grad_from_pre, grad_gain_pre = norm_backward(grad_pre, pre_unit, pre_inv, norm_pre)
    grad_residual = grad_out + grad_from_pre
    grad_branch_full, grad_gain_attn = norm_backward(grad_residual, attn_unit, attn_inv, norm_attn)
    grad_branch = grad_branch_full.astype(low)
    term_output = jnp.einsum("tc,td->cd", attended, grad_branch, preferred_element_type=f32)
    grad_attended = jnp.einsum(
        "td,cd->tc", grad_branch, full_output, preferred_element_type=f32
    ).astype(low)
    grad_heads = grad_attended.reshape(local, H, HD)
    attended_heads = attended.reshape(local, H, HD)
    delta = jnp.transpose(jnp.sum(grad_heads.astype(f32) * attended_heads.astype(f32), axis=-1))[
        :, :, None
    ]
    grad_probs = jnp.einsum("qhd,kd->hqk", grad_heads, value_all, preferred_element_type=f32)
    grad_scores = (probs_full * (grad_probs - delta)).astype(low)
    value_term = jnp.einsum("hqk,qhd->kd", probs, grad_heads, preferred_element_type=f32)
    key_term = jnp.einsum("hqk,qhd->kd", grad_scores, query_rot, preferred_element_type=f32)
    key_value_terms = jnp.concatenate([key_term, value_term], axis=1)
    grad_query_rot = jnp.einsum("hqk,kd->qhd", grad_scores, key_all, preferred_element_type=f32)
    summed_kv = lax.psum_scatter(
        key_value_terms.astype(jnp.bfloat16), "ctx", scatter_dimension=0, tiled=True
    ).astype(jnp.float32)
    grad_key_rot = summed_kv[:, :HD]
    grad_values = summed_kv[:, HD:].astype(low)
    grad_q_normed = rotate_back(grad_query_rot * scale, cosine[:, None, :], sine[:, None, :])
    grad_q_full, grad_gain_query = norm_backward(grad_q_normed, query_unit, query_inv, norm_query)
    grad_k_normed = rotate_back(grad_key_rot, cosine, sine)
    grad_k_full, grad_gain_key = norm_backward(grad_k_normed, key_unit, key_inv, norm_key)
    grad_q_in = grad_q_full.reshape(local, H * HD).astype(low)
    grad_k_in = grad_k_full.astype(low)
    term_query = jnp.einsum("td,tc->dc", normed_in, grad_q_in, preferred_element_type=f32)
    term_key = jnp.einsum("td,tc->dc", normed_in, grad_k_in, preferred_element_type=f32)
    term_value = jnp.einsum("td,tc->dc", normed_in, grad_values, preferred_element_type=f32)
    grad_normed = (
        jnp.einsum("tc,dc->td", grad_q_in, full_query, preferred_element_type=f32)
        + jnp.einsum("tc,dc->td", grad_k_in, full_key, preferred_element_type=f32)
        + jnp.einsum("tc,dc->td", grad_values, full_value, preferred_element_type=f32)
    )
    grad_from_in, grad_gain_in = norm_backward(grad_normed, unit_in, inv_in, norm_in)
    in_grad = (grad_residual + grad_from_in).astype(low)
    shards = (
        lax.psum_scatter(
            term_query.astype(jnp.bfloat16), "fsdp", scatter_dimension=0, tiled=True
        ).astype(jnp.float32),
        lax.psum_scatter(
            term_key.astype(jnp.bfloat16), "fsdp", scatter_dimension=0, tiled=True
        ).astype(jnp.float32),
        lax.psum_scatter(
            term_value.astype(jnp.bfloat16), "fsdp", scatter_dimension=0, tiled=True
        ).astype(jnp.float32),
        lax.psum_scatter(
            term_output.astype(jnp.bfloat16), "fsdp", scatter_dimension=1, tiled=True
        ).astype(jnp.float32),
        lax.psum_scatter(
            grad_gain_in.astype(jnp.bfloat16), "fsdp", scatter_dimension=0, tiled=True
        ).astype(jnp.float32),
        lax.psum_scatter(
            grad_gain_query.astype(jnp.bfloat16), "fsdp", scatter_dimension=0, tiled=True
        ).astype(jnp.float32),
        lax.psum_scatter(
            grad_gain_key.astype(jnp.bfloat16), "fsdp", scatter_dimension=0, tiled=True
        ).astype(jnp.float32),
        lax.psum_scatter(
            grad_gain_attn.astype(jnp.bfloat16), "fsdp", scatter_dimension=0, tiled=True
        ).astype(jnp.float32),
        lax.psum_scatter(
            grad_gain_pre.astype(jnp.bfloat16), "fsdp", scatter_dimension=0, tiled=True
        ).astype(jnp.float32),
        lax.psum_scatter(
            grad_gain_post.astype(jnp.bfloat16), "fsdp", scatter_dimension=0, tiled=True
        ).astype(jnp.float32),
    )
    totals = (
        lax.psum(shards[0].astype(jnp.bfloat16), "ctx").astype(jnp.float32),
        lax.psum(shards[1].astype(jnp.bfloat16), "ctx").astype(jnp.float32),
        lax.psum(shards[2].astype(jnp.bfloat16), "ctx").astype(jnp.float32),
        lax.psum(shards[3].astype(jnp.bfloat16), "ctx").astype(jnp.float32),
        lax.psum(shard_gate.astype(jnp.bfloat16), "ctx").astype(jnp.float32),
        lax.psum(shard_up.astype(jnp.bfloat16), "ctx").astype(jnp.float32),
        lax.psum(shard_down.astype(jnp.bfloat16), "ctx").astype(jnp.float32),
        lax.psum(shards[4].astype(jnp.bfloat16), "ctx").astype(jnp.float32),
        lax.psum(shards[5].astype(jnp.bfloat16), "ctx").astype(jnp.float32),
        lax.psum(shards[6].astype(jnp.bfloat16), "ctx").astype(jnp.float32),
        lax.psum(shards[7].astype(jnp.bfloat16), "ctx").astype(jnp.float32),
        lax.psum(shards[8].astype(jnp.bfloat16), "ctx").astype(jnp.float32),
        lax.psum(shards[9].astype(jnp.bfloat16), "ctx").astype(jnp.float32),
    )
    return (
        outputs[None],
        in_grad[None],
        totals[0],
        totals[1],
        totals[2],
        totals[3],
        totals[4],
        totals[5],
        totals[6],
        totals[7],
        totals[8],
        totals[9],
        totals[10],
        totals[11],
        totals[12],
    )


def solution(mesh):
    placed = (
        P("fsdp", "ctx", None),
        P("fsdp", "ctx", None),
        P("fsdp", "ctx"),
        P(),
        P("fsdp", None),
        P("fsdp", None),
        P("fsdp", None),
        P(None, "fsdp"),
        P("fsdp", None),
        P("fsdp", None),
        P("fsdp", None),
        P("fsdp"),
        P("fsdp"),
        P("fsdp"),
        P("fsdp"),
        P("fsdp"),
        P("fsdp"),
    )
    return jax.shard_map(
        body,
        mesh=mesh,
        in_specs=placed,
        out_specs=(
            P("fsdp", "ctx", None),
            P("fsdp", "ctx", None),
            P("fsdp", None),
            P("fsdp", None),
            P("fsdp", None),
            P(None, "fsdp"),
            P("fsdp", None),
            P("fsdp", None),
            P("fsdp", None),
            P("fsdp"),
            P("fsdp"),
            P("fsdp"),
            P("fsdp"),
            P("fsdp"),
            P("fsdp"),
        ),
        check_vma=False,
    )
```

profile of v0, /device:TPU:8, one launch (start us, length us, event | category | flops | bytes accessed | tf_op | source)
XLA Modules:
  0.0 1100.2 jit_solution(11387176566763124986)
XLA Ops:
  8.8 1.3 fusion.101
  11.4 1.1 fusion.43
  18.5 65.3 %all-reduce.13 = (bf16[1152]{0:T(1024)(128)(2,1)S(1)}, bf16[256]{0:T(256)(128)(2,1)S(1)}, bf16[256]{0:T(256)(128)(2,1)S(1)}, bf16[1152]{0:T(1024)(128)(2,1)S(1)}...) all-reduce(bf16[1152]{0:T(1024)(128)(2,1)S(1)} %dynamic-update-slic, ...), channel_id=1, replica_groups=mesh['ctx'=8,'fsdp'=16] {'fsdp'}, use_global_device_ids=true, to_apply=%add | all-reduce | flops 5120 | bytes 20480
  83.8 26.9 %all_gather.45 = bf16[1152,256]{1,0:T(8,128)(2,1)S(1)} all-gather(bf16[72,256]{1,0:T(8,128)(2,1)} %param.22), channel_id=1, replica_groups=mesh['ctx'=8,'fsdp'=16] {'fsdp'}, dimensions={0}, use_global_device_ids=true | all-gather | bytes 626688 | tf_op jit(solution)/shard_map/all_gather | solution.py:98
  110.8 1.5 multiply_reduce_fusion.10
  113.2 29.1 %all_gather.47 = bf16[1024,256]{1,0:T(8,128)(2,1)S(1)} all-gather(bf16[128,256]{1,0:T(8,128)(2,1)S(1)} %pad_maximum_fusion.3), channel_id=1, replica_groups=mesh['ctx'=8,'fsdp'=16] {'ctx'}, dimensions={0}, use_global_device_ids=true | all-gather | bytes 589824 | tf_op jit(solution)/shard_map/all_gather | solution.py:134
  142.3 21.9 %all_gather.43 = bf16[1152,256]{1,0:T(8,128)(2,1)S(1)} all-gather(bf16[72,256]{1,0:T(8,128)(2,1)S(1)} %copy-done.39), channel_id=1, replica_groups=mesh['ctx'=8,'fsdp'=16] {'fsdp'}, dimensions={0}, use_global_device_ids=true | all-gather | bytes 626688 | tf_op jit(solution)/shard_map/all_gather | solution.py:99
  165.3 29.2 %all_gather.44 = bf16[1024,256]{1,0:T(8,128)(2,1)S(1)} all-gather(bf16[128,256]{1,0:T(8,128)(2,1)S(1)} %convolution_convert_fusion.10), channel_id=1, replica_groups=mesh['ctx'=8,'fsdp'=16] {'ctx'}, dimensions={0}, use_global_device_ids=true | all-gather | bytes 589824 | tf_op jit(solution)/shard_map/all_gather | solution.py:135
  194.6 4.5 copy.77
  199.0 2.6 multiply_reduce_fusion.7
  203.5 0.9 copy-done.5
  205.1 2.7 multiply_reduce_fusion.3
  209.2 55.1 %all-gather.9.cloned.1.call-done = bf16[2048,1152]{1,0:T(8,128)(2,1)} async-done(((bf16[128,1152]{1,0:T(8,128)(2,1)}), bf16[2048,1152]{1,0:T(8,128)(2,1)}) %all-gather.9.cloned.1.call-update) | async-done | bytes 4718608 | tf_op jit(solution)/shard_map/all_gather | solution.py:154
  264.3 5.2 fusion.102
  269.6 4.6 multiply_convert_fusion.1
  274.3 1.2 copy-done.53
  275.5 4.6 convolution_convert_fusion
  280.2 81.5 %reduce-scatter.8.cloned.1.call-done = bf16[128,1152]{1,0:T(8,128)(2,1)} async-done(((bf16[2048,1152]{1,0:T(8,128)(2,1)}), bf16[128,1152]{1,0:T(8,128)(2,1)}) %reduce-scatter.8.cloned.1.call-update) | async-done | bytes 294928 | tf_op jit(solution)/shard_map/reduce_scatter | solution.py:159
  361.7 1.1 fusion.34
  362.8 1.3 fusion.46
  364.1 1.9 fusion.28
  366.3 56.5 %all-gather.11.cloned.1.call-done = bf16[2048,1152]{1,0:T(8,128)(2,1)} async-done(((bf16[128,1152]{1,0:T(8,128)(2,1)}), bf16[2048,1152]{1,0:T(8,128)(2,1)}) %all-gather.11.cloned.1.call-update) | async-done | bytes 4718608 | tf_op jit(solution)/shard_map/all_gather | solution.py:170
  422.8 8.5 multiply_convert_fusion
  431.4 3.0 fusion.103
  434.4 4.6 add_convert_fusion
  439.1 81.6 %reduce-scatter.10.cloned.1.call-done = bf16[128,1152]{1,0:T(8,128)(2,1)} async-done(((bf16[2048,1152]{1,0:T(8,128)(2,1)}), bf16[128,1152]{1,0:T(8,128)(2,1)}) %reduce-scatter.10.cloned.1.call-update) | async-done | bytes 294928 | tf_op jit(solution)/shard_map/reduce_scatter | solution.py:177
  520.7 1.3 fusion.35
  522.0 2.3 multiply_reduce_fusion
  524.5 1.2 convolution_convert_fusion.8
  525.8 1.8 copy.80
  527.6 1.2 multiply_reduce_fusion.6
  528.8 1.5 fusion.12
  531.0 1.0 copy-done.23
  532.5 1.1 pad_maximum_fusion
  533.6 38.6 %reduce-scatter.12.cloned.1.call-done = bf16[128,512]{1,0:T(8,128)(2,1)} async-done(((bf16[1024,512]{1,0:T(8,128)(2,1)}), bf16[128,512]{1,0:T(8,128)(2,1)}) %reduce-scatter.12.cloned.1.call-update) | async-done | bytes 131088 | tf_op jit(solution)/shard_map/reduce_scatter | solution.py:205
  572.3 2.1 convolution_convert_fusion.6
  574.4 0.9 convert_element_type.275
  576.0 1.2 convolution_convert_fusion.7
  577.3 2.2 convolution_convert_fusion.1
  581.4 2.4 convolution_convert_fusion.2
  585.2 6.5 convolution_convert_fusion.3
  591.7 3.4 convolution_convert_fusion.4
  595.1 0.9 fusion.104
  597.0 60.0 %all-reduce.12 = (bf16[1152]{0:T(1024)(128)(2,1)S(1)}, bf16[256]{0:T(256)(128)(2,1)S(1)}, bf16[256]{0:T(256)(128)(2,1)S(1)}, bf16[1152]{0:T(1024)(128)(2,1)S(1)}...) all-reduce(bf16[1152]{0:T(1024)(128)(2,1)S(1)} %get-tuple-element.2, ...), channel_id=9, replica_groups=mesh['ctx'=8,'fsdp'=16] {'fsdp'}, use_global_device_ids=true, to_apply=%region_32.33.clone | all-reduce | flops 5120 | bytes 20480
  660.5 45.4 %reduce-scatter.16.cloned.1.call-done = bf16[72,256]{1,0:T(8,128)(2,1)} async-done(((bf16[1152,256]{1,0:T(8,128)(2,1)}), bf16[72,256]{1,0:T(8,128)(2,1)}) %reduce-scatter.16.cloned.1.call-update) | async-done | bytes 36880 | tf_op jit(solution)/shard_map/reduce_scatter | solution.py:230
  706.0 6.3 convolution_convert_fusion.5
  712.3 68.7 %reduce-scatter.20.cloned.1.call-done = bf16[1024,72]{0,1:T(8,128)(2,1)} async-done(((bf16[1024,1152]{0,1:T(8,128)(2,1)}), bf16[1024,72]{0,1:T(8,128)(2,1)}) %reduce-scatter.20.cloned.1.call-update) | async-done | bytes 147472 | tf_op jit(solution)/shard_map/reduce_scatter | solution.py:236
  781.0 75.3 %reduce-scatter.14.cloned.1.call-done = bf16[72,1024]{1,0:T(8,128)(2,1)} async-done(((bf16[1152,1024]{1,0:T(8,128)(2,1)}), bf16[72,1024]{1,0:T(8,128)(2,1)}) %reduce-scatter.14.cloned.1.call-update) | async-done | bytes 147472 | tf_op jit(solution)/shard_map/reduce_scatter | solution.py:227
  856.4 0.9 fusion.53
  857.3 71.0 %all-reduce.19.cloned.1.call-done = (bf16[72,256]{1,0:T(8,128)(2,1)}, bf16[72,256]{1,0:T(8,128)(2,1)}, bf16[72]{0:T(256)(128)(2,1)}, bf16[16]{0:T(256)(128)(2,1)...) async-done(((bf16[72,256]{1,0:T(8,128)(2,1)}, bf16[72,256]{1,0:T(8,128)(2,1)}, bf16[72]{0:T(256)(128)(2,1)}, ...) | async-done | bytes 74384 | tf_op jit(solution)/shard_map/psum | solution.py:260
  928.3 1.1 convert_element_type.293
  929.4 1.2 convert_element_type.295
  930.6 1.2 convert_element_type.297
  931.8 1.1 convert_element_type.299
  932.9 1.1 convert_element_type.301
  934.0 1.2 convert_element_type.303
  935.2 1.4 convert_element_type.281
  936.6 1.4 convert_element_type.283
  938.0 146.8 %all-reduce.21.cloned.1.call-done = (bf16[72,1024]{1,0:T(8,128)(2,1)}, bf16[1024,72]{0,1:T(8,128)(2,1)}, bf16[432,1152]{1,0:T(8,128)(2,1)}, bf16[432,1152]{1,0:T(8,128)(2,1)}, bf16[432,1152]{1,0:T(8,128)(2,1)}) async-done(((bf16[72,1024]{1,0:T(8,128)(2,1)}, bf16[1024,72]{0,1:T(8,128)(2,1)}, bf16[432,1152]{1,0:T(8,128)(2,1)}, bf16[432,1152]{1,0:T(8,128)(2,1)}, bf16[432,1152]{1,0:T(8,128)(2,1)}), ...) | async-done | bytes 3280912 | tf_op jit(solution)/shard_map/psum | solution.py:259
  1084.8 1.7 convert_element_type.279
  1086.5 1.6 convert_element_type.285
  1088.1 2.7 convert_element_type.287
  1090.8 1.4 convert_element_type.289
  1092.2 1.4 convert_element_type.291
  (211 shorter events, 22.1 us)
Async XLA Ops:
  7.2 268.3 %copy-start = (bf16[432,1152]{1,0:T(8,128)(2,1)S(1)}, bf16[432,1152]{1,0:T(8,128)(2,1)}, u32[]{:S(2)}) copy-start(bf16[432,1152]{1,0:T(8,128)(2,1)} %param.27) | copy-start | bytes 2985988
  7.2 157.8 %copy-start.2 = (bf16[1,128,1152]{2,1,0:T(8,128)(2,1)S(1)}, bf16[1,128,1152]{2,1,0:T(8,128)(2,1)}, u32[]{:S(2)}) copy-start(bf16[1,128,1152]{2,1,0:T(8,128)(2,1)} %param.17) | copy-start | bytes 884740
  7.2 105.3 %copy-start.48 = (s32[1,128]{1,0:T(1,128)S(1)}, s32[1,128]{1,0:T(1,128)}, u32[]{:S(2)}) copy-start(s32[1,128]{1,0:T(1,128)} %param.19) | copy-start | bytes 1540
  7.2 135.1 %copy-start.39 = (bf16[72,256]{1,0:T(8,128)(2,1)S(1)}, bf16[72,256]{1,0:T(8,128)(2,1)}, u32[]{:S(2)}) copy-start(bf16[72,256]{1,0:T(8,128)(2,1)} %param.23) | copy-start | bytes 110596
  7.2 187.3 %all-gather.5.cloned.1.call-start = ((), (), s32[]{:S(2)}) async-start(), calls=%async_computation.7 | async-start | bytes 2506752 | tf_op jit(solution)/shard_map/all_gather | solution.py:97
  8.0 197.1 %all-gather.7.cloned.1.call-start = ((), (), s32[]{:S(2)}) async-start(), calls=%async_computation.8 | async-start | bytes 2506752 | tf_op jit(solution)/shard_map/all_gather | solution.py:100
  8.7 255.6 %all-gather.9.cloned.1.call-start = ((), (), s32[]{:S(2)}) async-start(), calls=%async_computation.9 | async-start | bytes 5013504 | tf_op jit(solution)/shard_map/all_gather | solution.py:154
  110.7 2.3 copy-start.15
  112.3 53.1 %copy-start.21 = (f32[128,256]{1,0:T(8,128)}, f32[128,256]{1,0:T(8,128)S(1)}, u32[]{:S(2)}) copy-start(f32[128,256]{1,0:T(8,128)S(1)} %get-tuple-element.73) | copy-start | bytes 393220
  112.5 86.5 %copy-start.40 = (f32[128]{0:T(128)}, f32[128]{0:T(128)S(1)}, u32[]{:S(2)}) copy-start(f32[128]{0:T(128)S(1)} %convert_bitcast_fusion.1) | copy-start | bytes 1540
  112.8 89.0 %copy-start.32 = (f32[128,128]{1,0:T(8,128)}, f32[128,128]{1,0:T(8,128)S(1)}, u32[]{:S(2)}) copy-start(f32[128,128]{1,0:T(8,128)S(1)} %get-tuple-element.66) | copy-start | bytes 196612
  112.9 89.0 %copy-start.34 = (f32[128,128]{1,0:T(8,128)}, f32[128,128]{1,0:T(8,128)S(1)}, u32[]{:S(2)}) copy-start(f32[128,128]{1,0:T(8,128)S(1)} %get-tuple-element.67) | copy-start | bytes 196612
  142.3 60.2 %copy-start.12 = (bf16[1024,256]{1,0:T(8,128)(2,1)}, bf16[1024,256]{1,0:T(8,128)(2,1)S(1)}, u32[]{:S(2)}) copy-start(bf16[1024,256]{1,0:T(8,128)(2,1)S(1)} %all_gather.47) | copy-start | bytes 1572868
  194.6 8.9 copy-start.36
  202.0 1.5 copy-start.26
  202.0 1.5 copy-start.28
  203.0 1.4 copy-start.5
  204.4 3.4 copy-start.42
  205.0 2.8 copy-start.19
  209.0 152.7 %reduce-scatter.8.cloned.1.call-start = ((), (), s32[]{:S(2)}) async-start(), calls=%async_computation.10 | async-start | bytes 5013504 | tf_op jit(solution)/shard_map/reduce_scatter | solution.py:159
  264.3 5.3 copy-start.44
  264.3 5.3 copy-start.46
  269.6 4.6 copy-start.52
  274.3 1.2 copy-start.53
  280.1 82.7 %copy-start.14 = (bf16[1,128,1152]{2,1,0:T(8,128)(2,1)S(1)}, bf16[1,128,1152]{2,1,0:T(8,128)(2,1)}, u32[]{:S(2)}) copy-start(bf16[1,128,1152]{2,1,0:T(8,128)(2,1)} %param.18) | copy-start | bytes 884740
  280.1 142.7 %all-gather.11.cloned.1.call-start = ((), (), s32[]{:S(2)}) async-start(), calls=%async_computation.11 | async-start | bytes 5013504 | tf_op jit(solution)/shard_map/all_gather | solution.py:170
  366.0 154.7 %reduce-scatter.10.cloned.1.call-start = ((), (), s32[]{:S(2)}) async-start(), calls=%async_computation.12 | async-start | bytes 5013504 | tf_op jit(solution)/shard_map/reduce_scatter | solution.py:177
  422.8 8.6 copy-start.45
  431.4 3.0 copy-start.49
  431.4 3.0 copy-start.50
  431.4 3.0 copy-start.47
  439.1 82.9 %copy-start.11 = (bf16[128,1152]{1,0:T(8,128)(2,1)S(1)}, bf16[128,1152]{1,0:T(8,128)(2,1)}, u32[]{:S(2)}) copy-start(bf16[128,1152]{1,0:T(8,128)(2,1)} %reduce-scatter.8.cloned.1.call-done) | copy-start | bytes 884740
  439.1 133.2 %reduce-scatter.12.cloned.1.call-start = ((), (), s32[]{:S(2)}) async-start(), calls=%async_computation.13 | async-start | bytes 1179648 | tf_op jit(solution)/shard_map/reduce_scatter | solution.py:205
  522.0 2.5 copy-start.4
  524.3 3.2 copy-start.9
  524.3 4.4 copy-start.43
  524.5 4.2 copy-start.6
  527.6 2.7 copy-start.25
  527.6 2.8 copy-start.37
  530.3 1.7 copy-start.27
  530.3 1.7 copy-start.29
  532.4 42.9 %copy-start.41 = (f32[128]{0:T(128)S(1)}, f32[128]{0:T(128)}, u32[]{:S(2)}) copy-start(f32[128]{0:T(128)} %copy-done.40) | copy-start | bytes 1540
  532.4 43.2 %copy-start.22 = (f32[128,256]{1,0:T(8,128)S(1)}, f32[128,256]{1,0:T(8,128)}, u32[]{:S(2)}) copy-start(f32[128,256]{1,0:T(8,128)} %copy-done.21) | copy-start | bytes 393220
  533.5 43.8 %copy-start.20 = (bf16[256,4,128]{2,0,1:T(8,128)(2,1)S(1)}, bf16[256,4,128]{2,0,1:T(8,128)(2,1)}, u32[]{:S(2)}) copy-start(bf16[256,4,128]{2,0,1:T(8,128)(2,1)} %copy-done.19) | copy-start | bytes 786436
  533.6 127.0 %reduce-scatter.18.cloned.1.call-start = ((), (), s32[]{:S(2)}) async-start(), calls=%async_computation.16 | async-start | bytes 626688 | tf_op jit(solution)/shard_map/reduce_scatter | solution.py:233
  574.4 131.6 %reduce-scatter.16.cloned.1.call-start = ((), (), s32[]{:S(2)}) async-start(), calls=%async_computation.15 | async-start | bytes 626688 | tf_op jit(solution)/shard_map/reduce_scatter | solution.py:230
  577.2 2.6 copy-start.13
  577.2 2.6 copy-start.24
  577.3 203.8 %reduce-scatter.20.cloned.1.call-start = ((), (), s32[]{:S(2)}) async-start(), calls=%async_computation.17 | async-start | bytes 2506752 | tf_op jit(solution)/shard_map/reduce_scatter | solution.py:236
  579.5 1.1 copy-start.8
  579.6 276.8 %reduce-scatter.14.cloned.1.call-start = ((), (), s32[]{:S(2)}) async-start(), calls=%async_computation.14 | async-start | bytes 2506752 | tf_op jit(solution)/shard_map/reduce_scatter | solution.py:227
  583.7 7.9 slice-start
  583.7 344.6 %all-reduce.19.cloned.1.call-start = ((), (), s32[]{:S(2)}) async-start(), calls=%async_computation.18 | async-start | bytes 153600 | tf_op jit(solution)/shard_map/psum | solution.py:260
  585.1 6.5 slice-start.1
  585.1 6.5 copy-start.51
  591.7 3.4 copy-start.3
  595.1 1.1 copy-start.16
  595.1 1.4 copy-start.18
  595.1 1.4 copy-start.38
  706.0 378.8 %all-reduce.21.cloned.1.call-start = ((), (), s32[]{:S(2)}) async-start(), calls=%async_computation.19 | async-start | bytes 6561792 | tf_op jit(solution)/shard_map/psum | solution.py:259
  712.3 144.1 %copy-start.10 = (f32[128,1152]{1,0:T(8,128)S(1)}, f32[128,1152]{1,0:T(8,128)}, u32[]{:S(2)}) copy-start(f32[128,1152]{1,0:T(8,128)} %copy-done.9) | copy-start | bytes 1769476
  1084.7 6.1 copy-start.31
  1088.1 4.1 copy-start.30
  1090.8 2.8 copy-start.1
  (5 other events, 4.5 us)
Sparse Core Ops, SparseCore 0:
  10.5 51.5 all-gather.4
  64.5 49.3 all-gather.6
  209.1 55.2 all-gather.8
  280.3 81.4 reduce-scatter.7
  366.2 56.6 all-gather.10
  439.2 81.4 reduce-scatter.9
  533.7 38.5 reduce-scatter.11
  576.0 62.8 reduce-scatter.17
  642.6 63.2 reduce-scatter.15
  709.8 71.2 reduce-scatter.19
  785.0 71.2 reduce-scatter.13
  859.8 68.4 all-reduce.18
  932.1 152.6 all-reduce.20
where the time goes:
time: 1100 us
  waiting for transfers between devices  722 us (66%)
  blocking collectives  232 us (21%)
  matrix products  69.1 us (6%)
  other arithmetic  35.6 us (3%)
  local copies, waits for them, and re-layouts  22.2 us (2%)
  between operations  17.4 us (2%)
    psum x1, waiting for transfers between devices, body(): lax.psum(shards[0].astype(jnp.bfloat16), 'ctx').astype(jnp.float32)  147 us
    unnamed x2, blocking collectives  125 us
    reduce_scatter x1, waiting for transfers between devices, body(): lax.psum_scatter((jnp.dot(grad_gate, w_gate, preferred_element_type=f32)...  81.6 us
    reduce_scatter x1, waiting for transfers between devices, body(): lax.psum_scatter(jnp.dot(hidden, w_down, preferred_element_type=f32).asty...  81.5 us
    reduce_scatter x1, waiting for transfers between devices, body(): lax.psum_scatter(term_query.astype(jnp.bfloat16), 'fsdp', scatter_dimensi...  75.3 us
    psum x1, waiting for transfers between devices, body(): lax.psum(shards[1].astype(jnp.bfloat16), 'ctx').astype(jnp.float32)  71 us
    reduce_scatter x1, waiting for transfers between devices, body(): lax.psum_scatter(term_output.astype(jnp.bfloat16), 'fsdp', scatter_dimens...  68.7 us
    all_gather x1, waiting for transfers between devices, body(): grad_all = lax.all_gather(grad_ffn, 'fsdp', axis=0, tiled=True)  56.5 us
  transfers between devices with their start and end apart: 13, of which 10 were waited for; matrix products, arithmetic and copies ran while one was open for 5% of the time, Pallas kernels for 0%

commit v1 on v0

--- a/solution.py
+++ b/solution.py
@@ -257,7 +257,7 @@
     )
     totals = (
         lax.psum(shards[0].astype(jnp.bfloat16), "ctx").astype(jnp.float32),
-        lax.psum(shards[1].astype(jnp.bfloat16), "ctx").astype(jnp.float32),
+        jnp.sum(lax.all_gather(shards[1].astype(jnp.bfloat16), "ctx"), axis=0).astype(jnp.float32),
         lax.psum(shards[2].astype(jnp.bfloat16), "ctx").astype(jnp.float32),
         lax.psum(shards[3].astype(jnp.bfloat16), "ctx").astype(jnp.float32),
         lax.psum(shard_gate.astype(jnp.bfloat16), "ctx").astype(jnp.float32),

time: 1100 us -> 1030 us (0.936)
  waiting for transfers between devices: 722 us -> 589 us
  blocking collectives: 232 us -> 301 us
    psum x1 -> x0, waiting for transfers between devices: 71 us -> none  [body(): lax.psum(shards[1].astype(jnp.bfloat16), 'ctx').astype(jnp.float32)]
    psum x0 -> x1, blocking collectives: none -> 34.2 us  [body(): lax.psum(shards[2].astype(jnp.bfloat16), 'ctx').astype(jnp.float32)]
    all_gather x0 -> x1, blocking collectives: none -> 33.5 us  [body(): lax.all_gather(shards[1].astype(jnp.bfloat16), 'ctx')]
    psum x1, waiting for transfers between devices: 147 us -> 125 us  [body(): lax.psum(shards[0].astype(jnp.bfloat16), 'ctx').astype(jnp.float32)]
    reduce_scatter x1, waiting for transfers between devices: 45.4 us -> 29 us  [body(): lax.psum_scatter(term_key.astype(jnp.bfloat16), 'fsdp', scatter_dimension...]
    reduce_scatter x1, waiting for transfers between devices: 38.6 us -> 26.3 us  [body(): lax.psum_scatter(key_value_terms.astype(jnp.bfloat16), 'ctx', scatter_dim...]
    reduce_scatter x1, waiting for transfers between devices: 68.7 us -> 57.3 us  [body(): lax.psum_scatter(term_output.astype(jnp.bfloat16), 'fsdp', scatter_dimens...]
  transfers between devices with their start and end apart: 13 -> 12, of which waited for: 10 -> 9; matrix products, arithmetic and copies ran while one was open for 5% -> 6% of each run, Pallas kernels for 0% -> 0%
where the time goes in v1:
time: 1030 us
  waiting for transfers between devices  589 us (57%)
  blocking collectives  301 us (29%)
  matrix products  72.8 us (7%)
  other arithmetic  30.4 us (3%)
  local copies, waits for them, and re-layouts  19 us (2%)
  between operations  17.8 us (2%)
    unnamed x2, blocking collectives  126 us
    psum x1, waiting for transfers between devices, body(): lax.psum(shards[0].astype(jnp.bfloat16), 'ctx').astype(jnp.float32)  125 us
    reduce_scatter x1, waiting for transfers between devices, body(): lax.psum_scatter((jnp.dot(grad_gate, w_gate, preferred_element_type=f32)...  81.6 us
    reduce_scatter x1, waiting for transfers between devices, body(): lax.psum_scatter(jnp.dot(hidden, w_down, preferred_element_type=f32).asty...  81.5 us
    reduce_scatter x1, waiting for transfers between devices, body(): lax.psum_scatter(term_query.astype(jnp.bfloat16), 'fsdp', scatter_dimensi...  75.1 us
    reduce_scatter x1, waiting for transfers between devices, body(): lax.psum_scatter(term_output.astype(jnp.bfloat16), 'fsdp', scatter_dimens...  57.3 us
    all_gather x1, waiting for transfers between devices, body(): grad_all = lax.all_gather(grad_ffn, 'fsdp', axis=0, tiled=True)  56.5 us
    all_gather x1, waiting for transfers between devices, body(): rows_all = lax.all_gather(normed_pre, 'fsdp', axis=0, tiled=True)  55.1 us
  transfers between devices with their start and end apart: 12, of which 9 were waited for; matrix products, arithmetic and copies ran while one was open for 6% of the time, Pallas kernels for 0%

profile of v1, /device:TPU:8, one launch (start us, length us, event | category | flops | bytes accessed | tf_op | source)
XLA Modules:
  0.0 1030.7 jit_solution(13307943117095789618)
XLA Ops:
  8.8 1.3 fusion.101
  11.4 1.1 fusion.43
  13.4 0.9 dynamic-update-slice.1
  14.3 0.8 dynamic-update-slice.2
  15.1 0.8 dynamic-update-slice.4
  16.0 0.8 dynamic-update-slice.3
  16.8 0.8 dynamic-update-slice
  17.7 0.8 dynamic-update-slice.5
  18.5 65.3 %all-reduce.13 = (bf16[1152]{0:T(1024)(128)(2,1)S(1)}, bf16[256]{0:T(256)(128)(2,1)S(1)}, bf16[256]{0:T(256)(128)(2,1)S(1)}, bf16[1152]{0:T(1024)(128)(2,1)S(1)}...) all-reduce(bf16[1152]{0:T(1024)(128)(2,1)S(1)} %dynamic-update-slic, ...), channel_id=1, replica_groups=mesh['ctx'=8,'fsdp'=16] {'fsdp'}, use_global_device_ids=true, to_apply=%add | all-reduce | flops 5120 | bytes 20480
  83.8 26.9 %all_gather.51 = bf16[1152,256]{1,0:T(8,128)(2,1)S(1)} all-gather(bf16[72,256]{1,0:T(8,128)(2,1)} %param.22), channel_id=1, replica_groups=mesh['ctx'=8,'fsdp'=16] {'fsdp'}, dimensions={0}, use_global_device_ids=true | all-gather | bytes 626688 | tf_op jit(solution)/shard_map/all_gather | solution.py:98
  110.7 1.5 multiply_reduce_fusion.10
  113.2 29.1 %all_gather.53 = bf16[1024,256]{1,0:T(8,128)(2,1)S(1)} all-gather(bf16[128,256]{1,0:T(8,128)(2,1)S(1)} %pad_maximum_fusion.3), channel_id=1, replica_groups=mesh['ctx'=8,'fsdp'=16] {'ctx'}, dimensions={0}, use_global_device_ids=true | all-gather | bytes 589824 | tf_op jit(solution)/shard_map/all_gather | solution.py:134
  142.3 21.9 %all_gather.49 = bf16[1152,256]{1,0:T(8,128)(2,1)S(1)} all-gather(bf16[72,256]{1,0:T(8,128)(2,1)S(1)} %copy-done.38), channel_id=1, replica_groups=mesh['ctx'=8,'fsdp'=16] {'fsdp'}, dimensions={0}, use_global_device_ids=true | all-gather | bytes 626688 | tf_op jit(solution)/shard_map/all_gather | solution.py:99
  165.3 29.2 %all_gather.50 = bf16[1024,256]{1,0:T(8,128)(2,1)S(1)} all-gather(bf16[128,256]{1,0:T(8,128)(2,1)S(1)} %convolution_convert_fusion.10), channel_id=1, replica_groups=mesh['ctx'=8,'fsdp'=16] {'ctx'}, dimensions={0}, use_global_device_ids=true | all-gather | bytes 589824 | tf_op jit(solution)/shard_map/all_gather | solution.py:135
  194.6 4.5 copy.77
  199.1 2.6 multiply_reduce_fusion.7
  203.5 0.9 copy-done.4
  205.1 2.7 multiply_reduce_fusion.3
  208.1 0.8 multiply_convert_fusion.3
  209.2 55.1 %all-gather.10.cloned.1.call-done = bf16[2048,1152]{1,0:T(8,128)(2,1)} async-done(((bf16[128,1152]{1,0:T(8,128)(2,1)}), bf16[2048,1152]{1,0:T(8,128)(2,1)}) %all-gather.10.cloned.1.call-update) | async-done | bytes 4718608 | tf_op jit(solution)/shard_map/all_gather | solution.py:154
  264.4 5.2 fusion.102
  269.6 4.6 multiply_convert_fusion.1
  274.3 1.2 copy-done.52
  275.5 4.7 convolution_convert_fusion
  280.2 81.5 %reduce-scatter.8.cloned.1.call-done = bf16[128,1152]{1,0:T(8,128)(2,1)} async-done(((bf16[2048,1152]{1,0:T(8,128)(2,1)}), bf16[128,1152]{1,0:T(8,128)(2,1)}) %reduce-scatter.8.cloned.1.call-update) | async-done | bytes 294928 | tf_op jit(solution)/shard_map/reduce_scatter | solution.py:159
  361.7 1.1 fusion.34
  362.9 1.3 fusion.46
  364.1 1.9 fusion.28
  366.3 56.5 %all-gather.12.cloned.1.call-done = bf16[2048,1152]{1,0:T(8,128)(2,1)} async-done(((bf16[128,1152]{1,0:T(8,128)(2,1)}), bf16[2048,1152]{1,0:T(8,128)(2,1)}) %all-gather.12.cloned.1.call-update) | async-done | bytes 4718608 | tf_op jit(solution)/shard_map/all_gather | solution.py:170
  422.9 8.5 multiply_convert_fusion
  431.5 3.0 fusion.103
  434.5 4.6 add_convert_fusion
  439.2 81.6 %reduce-scatter.10.cloned.1.call-done = bf16[128,1152]{1,0:T(8,128)(2,1)} async-done(((bf16[2048,1152]{1,0:T(8,128)(2,1)}), bf16[128,1152]{1,0:T(8,128)(2,1)}) %reduce-scatter.10.cloned.1.call-update) | async-done | bytes 294928 | tf_op jit(solution)/shard_map/reduce_scatter | solution.py:177
  520.8 1.3 fusion.35
  522.0 2.3 multiply_reduce_fusion
  524.6 1.2 convolution_convert_fusion.8
  525.8 1.8 copy.80
  527.6 1.2 multiply_reduce_fusion.6
  528.8 1.5 fusion.12
  531.0 1.0 copy-done.22
  532.5 1.1 pad_maximum_fusion
  533.6 2.2 convolution_convert_fusion.1
  537.7 2.4 convolution_convert_fusion.2
  540.2 5.9 convolution_convert_fusion.3
  546.0 26.3 %reduce-scatter.12.cloned.1.call-done = bf16[128,512]{1,0:T(8,128)(2,1)} async-done(((bf16[1024,512]{1,0:T(8,128)(2,1)}), bf16[128,512]{1,0:T(8,128)(2,1)}) %reduce-scatter.12.cloned.1.call-update) | async-done | bytes 131088 | tf_op jit(solution)/shard_map/reduce_scatter | solution.py:205
  572.3 2.1 convolution_convert_fusion.6
  574.5 0.9 convert_element_type.277
  576.1 1.3 convolution_convert_fusion.7
  577.4 6.4 convolution_convert_fusion.4
  583.8 5.9 convolution_convert_fusion.5
  589.7 57.3 %reduce-scatter.20.cloned.1.call-done = bf16[1024,72]{0,1:T(8,128)(2,1)} async-done(((bf16[1024,1152]{0,1:T(8,128)(2,1)}), bf16[1024,72]{0,1:T(8,128)(2,1)}) %reduce-scatter.20.cloned.1.call-update) | async-done | bytes 147472 | tf_op jit(solution)/shard_map/reduce_scatter | solution.py:236
  647.0 75.1 %reduce-scatter.14.cloned.1.call-done = bf16[72,1024]{1,0:T(8,128)(2,1)} async-done(((bf16[1152,1024]{1,0:T(8,128)(2,1)}), bf16[72,1024]{1,0:T(8,128)(2,1)}) %reduce-scatter.14.cloned.1.call-update) | async-done | bytes 147472 | tf_op jit(solution)/shard_map/reduce_scatter | solution.py:227
  723.6 2.6 fusion.104
  727.0 60.8 %all-reduce.12 = (bf16[1152]{0:T(1024)(128)(2,1)S(1)}, bf16[256]{0:T(256)(128)(2,1)S(1)}, bf16[256]{0:T(256)(128)(2,1)S(1)}, bf16[1152]{0:T(1024)(128)(2,1)S(1)}...) all-reduce(bf16[1152]{0:T(1024)(128)(2,1)S(1)} %get-tuple-element.2, ...), channel_id=10, replica_groups=mesh['ctx'=8,'fsdp'=16] {'fsdp'}, use_global_device_ids=true, to_apply=%region_32.33.clone | all-reduce | flops 5120 | bytes 20480
  788.3 0.9 fusion.53
  789.2 34.2 %all-reduce.14 = (bf16[72,256]{1,0:T(8,128)(2,1)S(1)}, bf16[72]{0:T(256)(128)(2,1)S(1)}, bf16[16]{0:T(256)(128)(2,1)S(1)}, bf16[16]{0:T(256)(128)(2,1)S(1)}, bf1...) all-reduce(bf16[72,256]{1,0:T(8,128)(2,1)} %reduce-scatter.18.clone, ...), channel_id=1, replica_groups=mesh['ctx'=8,'fsdp'=16] {'ctx'}, use_global_device_ids=true, to_apply=%region_25.26 | all-reduce | flops 18752 | bytes 75008 | tf_op jit(solution)/shard_map/psum | solution.py:261
  827.1 29.0 %reduce-scatter.16.cloned.1.call-done = bf16[72,256]{1,0:T(8,128)(2,1)} async-done(((bf16[1152,256]{1,0:T(8,128)(2,1)}), bf16[72,256]{1,0:T(8,128)(2,1)}) %reduce-scatter.16.cloned.1.call-update) | async-done | bytes 36880 | tf_op jit(solution)/shard_map/reduce_scatter | solution.py:230
  856.1 33.5 %all-gather = bf16[576,256]{1,0:T(8,128)(2,1)S(1)} all-gather(bf16[72,256]{1,0:T(8,128)(2,1)} %reduce-scatter.16.cloned.1.call-done), channel_id=2, replica_groups=mesh['ctx'=8,'fsdp'=16] {'ctx'}, dimensions={0}, use_global_device_ids=true | all-gather | bytes 331776 | tf_op jit(solution)/shard_map/all_gather | solution.py:260
  890.2 124.8 %all-reduce.18.cloned.1.call-done = (bf16[72,1024]{1,0:T(8,128)(2,1)}, bf16[1024,72]{0,1:T(8,128)(2,1)}, bf16[432,1152]{1,0:T(8,128)(2,1)}, bf16[432,1152]{1,0:T(8,128)(2,1)}, bf16[432,1152]{1,0:T(8,128)(2,1)}) async-done(((bf16[72,1024]{1,0:T(8,128)(2,1)}, bf16[1024,72]{0,1:T(8,128)(2,1)}, bf16[432,1152]{1,0:T(8,128)(2,1)}, bf16[432,1152]{1,0:T(8,128)(2,1)}, bf16[432,1152]{1,0:T(8,128)(2,1)}), ...) | async-done | bytes 3280912 | tf_op jit(solution)/shard_map/psum | solution.py:259
  1015.0 1.7 convert_element_type.281
  1016.7 1.6 convert_element_type.287
  1018.4 2.7 convert_element_type.289
  1021.1 1.4 convert_element_type.291
  1022.5 1.4 convert_element_type.293
  (206 shorter events, 17.4 us)
Async XLA Ops:
  7.2 268.3 %copy-start = (bf16[432,1152]{1,0:T(8,128)(2,1)S(1)}, bf16[432,1152]{1,0:T(8,128)(2,1)}, u32[]{:S(2)}) copy-start(bf16[432,1152]{1,0:T(8,128)(2,1)} %param.27) | copy-start | bytes 2985988
  7.2 157.8 %copy-start.2 = (bf16[1,128,1152]{2,1,0:T(8,128)(2,1)S(1)}, bf16[1,128,1152]{2,1,0:T(8,128)(2,1)}, u32[]{:S(2)}) copy-start(bf16[1,128,1152]{2,1,0:T(8,128)(2,1)} %param.17) | copy-start | bytes 884740
  7.2 105.3 %copy-start.47 = (s32[1,128]{1,0:T(1,128)S(1)}, s32[1,128]{1,0:T(1,128)}, u32[]{:S(2)}) copy-start(s32[1,128]{1,0:T(1,128)} %param.19) | copy-start | bytes 1540
  7.2 135.1 %copy-start.38 = (bf16[72,256]{1,0:T(8,128)(2,1)S(1)}, bf16[72,256]{1,0:T(8,128)(2,1)}, u32[]{:S(2)}) copy-start(bf16[72,256]{1,0:T(8,128)(2,1)} %param.23) | copy-start | bytes 110596
  7.2 187.3 %all-gather.6.cloned.1.call-start = ((), (), s32[]{:S(2)}) async-start(), calls=%async_computation.7 | async-start | bytes 2506752 | tf_op jit(solution)/shard_map/all_gather | solution.py:97
  8.0 197.1 %all-gather.8.cloned.1.call-start = ((), (), s32[]{:S(2)}) async-start(), calls=%async_computation.8 | async-start | bytes 2506752 | tf_op jit(solution)/shard_map/all_gather | solution.py:100
  8.7 255.6 %all-gather.10.cloned.1.call-start = ((), (), s32[]{:S(2)}) async-start(), calls=%async_computation.9 | async-start | bytes 5013504 | tf_op jit(solution)/shard_map/all_gather | solution.py:154
  110.7 2.3 copy-start.14
  112.3 53.1 %copy-start.20 = (f32[128,256]{1,0:T(8,128)}, f32[128,256]{1,0:T(8,128)S(1)}, u32[]{:S(2)}) copy-start(f32[128,256]{1,0:T(8,128)S(1)} %get-tuple-element.72) | copy-start | bytes 393220
  112.5 86.6 %copy-start.39 = (f32[128]{0:T(128)}, f32[128]{0:T(128)S(1)}, u32[]{:S(2)}) copy-start(f32[128]{0:T(128)S(1)} %convert_bitcast_fusion.1) | copy-start | bytes 1540
  112.8 89.1 %copy-start.31 = (f32[128,128]{1,0:T(8,128)}, f32[128,128]{1,0:T(8,128)S(1)}, u32[]{:S(2)}) copy-start(f32[128,128]{1,0:T(8,128)S(1)} %get-tuple-element.65) | copy-start | bytes 196612
  112.8 89.1 %copy-start.33 = (f32[128,128]{1,0:T(8,128)}, f32[128,128]{1,0:T(8,128)S(1)}, u32[]{:S(2)}) copy-start(f32[128,128]{1,0:T(8,128)S(1)} %get-tuple-element.66) | copy-start | bytes 196612
  142.3 60.2 %copy-start.11 = (bf16[1024,256]{1,0:T(8,128)(2,1)}, bf16[1024,256]{1,0:T(8,128)(2,1)S(1)}, u32[]{:S(2)}) copy-start(bf16[1024,256]{1,0:T(8,128)(2,1)S(1)} %all_gather.53) | copy-start | bytes 1572868
  194.6 8.9 copy-start.35
  202.0 1.5 copy-start.25
  202.0 1.5 copy-start.27
  203.1 1.3 copy-start.4
  204.4 3.4 copy-start.41
  205.0 2.8 copy-start.18
  209.0 152.8 %reduce-scatter.8.cloned.1.call-start = ((), (), s32[]{:S(2)}) async-start(), calls=%async_computation.10 | async-start | bytes 5013504 | tf_op jit(solution)/shard_map/reduce_scatter | solution.py:159
  264.4 5.3 copy-start.43
  264.4 5.3 copy-start.45
  269.6 4.6 copy-start.51
  274.3 1.2 copy-start.52
  280.1 82.7 %copy-start.13 = (bf16[1,128,1152]{2,1,0:T(8,128)(2,1)S(1)}, bf16[1,128,1152]{2,1,0:T(8,128)(2,1)}, u32[]{:S(2)}) copy-start(bf16[1,128,1152]{2,1,0:T(8,128)(2,1)} %param.18) | copy-start | bytes 884740
  280.1 142.7 %all-gather.12.cloned.1.call-start = ((), (), s32[]{:S(2)}) async-start(), calls=%async_computation.11 | async-start | bytes 5013504 | tf_op jit(solution)/shard_map/all_gather | solution.py:170
  366.1 154.7 %reduce-scatter.10.cloned.1.call-start = ((), (), s32[]{:S(2)}) async-start(), calls=%async_computation.12 | async-start | bytes 5013504 | tf_op jit(solution)/shard_map/reduce_scatter | solution.py:177
  422.9 8.6 copy-start.44
  431.4 3.0 copy-start.48
  431.4 3.0 copy-start.50
  431.5 3.0 copy-start.46
  439.1 82.9 %copy-start.10 = (bf16[128,1152]{1,0:T(8,128)(2,1)S(1)}, bf16[128,1152]{1,0:T(8,128)(2,1)}, u32[]{:S(2)}) copy-start(bf16[128,1152]{1,0:T(8,128)(2,1)} %reduce-scatter.8.cloned.1.call-done) | copy-start | bytes 884740
  439.2 133.2 %reduce-scatter.12.cloned.1.call-start = ((), (), s32[]{:S(2)}) async-start(), calls=%async_computation.13 | async-start | bytes 1179648 | tf_op jit(solution)/shard_map/reduce_scatter | solution.py:205
  522.0 2.5 copy-start.3
  524.3 3.2 copy-start.8
  524.4 4.4 copy-start.42
  524.6 4.2 copy-start.5
  527.6 2.7 copy-start.24
  527.6 2.8 copy-start.36
  530.3 1.7 copy-start.26
  530.3 1.7 copy-start.28
  531.0 1.0 copy-start.22
  532.0 1.6 copy-start.19
  533.6 2.6 copy-start.12
  533.6 2.6 copy-start.23
  533.6 113.4 %reduce-scatter.20.cloned.1.call-start = ((), (), s32[]{:S(2)}) async-start(), calls=%async_computation.17 | async-start | bytes 2506752 | tf_op jit(solution)/shard_map/reduce_scatter | solution.py:236
  535.9 0.9 copy-start.32
  535.9 0.9 copy-start.34
  535.9 1.1 copy-start.7
  535.9 186.3 %reduce-scatter.14.cloned.1.call-start = ((), (), s32[]{:S(2)}) async-start(), calls=%async_computation.14 | async-start | bytes 2506752 | tf_op jit(solution)/shard_map/reduce_scatter | solution.py:227
  537.7 2.5 copy-start.53
  540.1 35.3 %copy-start.40 = (f32[128]{0:T(128)S(1)}, f32[128]{0:T(128)}, u32[]{:S(2)}) copy-start(f32[128]{0:T(128)} %copy-done.39) | copy-start | bytes 1540
  540.1 35.7 %copy-start.21 = (f32[128,256]{1,0:T(8,128)S(1)}, f32[128,256]{1,0:T(8,128)}, u32[]{:S(2)}) copy-start(f32[128,256]{1,0:T(8,128)} %copy-done.20) | copy-start | bytes 393220
  540.1 249.1 %reduce-scatter.18.cloned.1.call-start = ((), (), s32[]{:S(2)}) async-start(), calls=%async_computation.16 | async-start | bytes 626688 | tf_op jit(solution)/shard_map/reduce_scatter | solution.py:233
  574.4 281.7 %reduce-scatter.16.cloned.1.call-start = ((), (), s32[]{:S(2)}) async-start(), calls=%async_computation.15 | async-start | bytes 626688 | tf_op jit(solution)/shard_map/reduce_scatter | solution.py:230
  577.3 6.4 copy-start.49
  577.4 437.6 %all-reduce.18.cloned.1.call-start = ((), (), s32[]{:S(2)}) async-start(), calls=%async_computation.18 | async-start | bytes 6561792 | tf_op jit(solution)/shard_map/psum | solution.py:259
  722.2 4.0 copy-start.15
  723.5 3.0 copy-start.17
  723.6 3.0 copy-start.37
  726.2 62.1 %copy-start.9 = (f32[128,1152]{1,0:T(8,128)S(1)}, f32[128,1152]{1,0:T(8,128)}, u32[]{:S(2)}) copy-start(f32[128,1152]{1,0:T(8,128)} %copy-done.8) | copy-start | bytes 1769476
  1015.0 6.1 copy-start.30
  1018.4 4.1 copy-start.29
  1021.1 2.8 copy-start.1
  (2 other events, 1.7 us)
Sparse Core Ops, SparseCore 0:
  10.5 51.5 all-gather.5
  64.5 49.3 all-gather.7
  209.1 55.2 all-gather.9
  280.3 81.4 reduce-scatter.7
  366.2 56.6 all-gather.11
  439.3 81.4 reduce-scatter.9
  533.7 38.5 reduce-scatter.11
  576.3 70.6 reduce-scatter.19
  651.0 71.1 reduce-scatter.13
  725.8 63.2 reduce-scatter.17
  792.8 63.2 reduce-scatter.15
  860.0 154.9 all-reduce.17
